TPU v7x, 32 devices: a whole 2x2x4 slice. The times are simulated.
32 devices in a mesh: energy: 8 (over z, x), slab: 2 (over core), rep: 2 (over y).
Axes of the slice: x: 2, y: 2, z: 4, core: 2. Of those that a mesh axis runs over, the one named last changes fastest.
Arguments:
- green_blocks: bfloat16 [8, 2, 512, 512], P('energy', 'slab', 'rep'), may hold values from -1 to 1
- occupation: float32 [8], P('energy'), may hold values from 0.1 to 1
- offsets: int32 [2], replicated, may hold values from 1 to 4, as said below
- coulomb: float32 [2, 512, 512], P('slab', 'rep'), may hold values from -0.9 to 0.9
- hamiltonian: float32 [2, 512, 512], P('slab', 'rep'), may hold values from -0.25 to 0.25
- onsite_level: float32 [8], P('energy'), may hold values from 2 to 3
- green_steps: int32 [8], P('energy'), may hold values from 1 to 2, as said below
- screen_steps: int32 [2], replicated, may hold values from 0 to 2, as said below
Outputs:
- green_next: float32 [8, 2, 512, 512], P('energy', 'slab', 'rep')
- screened: bfloat16 [2, 2, 512, 512], P(None, 'slab', 'rep')
Inputs may be any that keep to these rules, and one draw needn't show every extreme that they name: `offsets`: some frequency has offset 4; every other frequency has a smaller one. `green_steps`: some energy takes 2 turns. `screen_steps`: some frequency takes 2 turns; every other frequency takes fewer.
All inputs are finite; a program needn't handle non-finite values.
Results may differ from a plain program's by a relative error of at most 0.0004.
Values may be sent and summed in bfloat16 or wider, within the bound.
No kernel may reach another device: no remote copies, remote signals or barrier semaphores. Data moves between devices by JAX's collectives and lax.ppermute only.
A program may use at most 64 MiB of HBM per device.

v0:
```python
import jax
import jax.numpy as jnp
from jax import lax
from jax.sharding import PartitionSpec as P

SHIFTS = 4
FREQS = 2
NG = 2
NW = 2
precise = lax.Precision.HIGHEST


def from_behind(block, axis, distance):
    devices = range(lax.axis_size(axis))
    route = [(i - distance, i) for i in devices if i - distance in devices]
    return lax.ppermute(block, axis, route)


def broadcast(block, axis, owner):
    block = jnp.where(lax.axis_index(axis) == owner, block, jnp.zeros_like(block))
    return lax.psum(block, axis)


def with_halo(value, sides, width):
    for axis, dim in sides:
        peers, length = (lax.axis_size(axis), value.shape[dim])
        up = [(i, (i + 1) % peers) for i in range(peers - 1)]
        down = [(j, i) for i, j in up]
        last = lax.slice_in_dim(value, length - width, length, axis=dim)
        first = lax.slice_in_dim(value, 0, width, axis=dim)
        before = lax.ppermute(last, axis, up)
        after = lax.ppermute(first, axis, down)
        value = jnp.concatenate([before, value, after], axis=dim)
    return value


def row_product(first_factor, second_factor):
    return jnp.einsum("esij,esjk->esik", first_factor, second_factor, precision=precise)


def full_rows(block_rows):
    return lax.all_gather(block_rows, "rep", axis=2, tiled=True)


def newton_rows(operator, initial, known_full, counts, turn_total):
    operator_full = lax.all_gather(operator, "rep", axis=2, tiled=True)
    iterate = initial
    for turn_index in range(turn_total):
        if turn_index == 0 and known_full is not None:
            iterate_full = known_full
        else:
            iterate_full = full_rows(iterate)
        composed = row_product(row_product(iterate, operator_full), iterate_full)
        iterate = jnp.where(
            (turn_index < counts)[:, None, None, None], 2.0 * iterate - composed, iterate
        )
    return iterate


def body(
    green_blocks, occupation, offsets, coulomb, hamiltonian, onsite_level, green_steps, screen_steps
):
    local_count, _, half_rows, full_width = green_blocks.shape
    energies = local_count * lax.axis_size("energy")
    entry_scale = full_width ** (-0.5)
    shift_count = -(-SHIFTS // local_count)
    pieces = []
    received = green_blocks
    for distance in range(1, shift_count + 1):
        received = from_behind(received, "energy", 1)
        pieces.insert(0, received)
    extended = jnp.concatenate(pieces + [green_blocks], axis=0)
    anchor = shift_count * local_count
    lowered = jnp.stack(
        [
            lax.dynamic_slice_in_dim(extended, anchor - offsets[index], local_count, 0)
            for index in range(FREQS)
        ]
    )
    lowered_wide = lowered.astype(jnp.float32)
    weighted = occupation[:, None, None, None] * green_blocks.astype(jnp.float32)
    partial_value = jnp.sum(weighted[None] * lowered_wide, axis=1) * energies ** (-0.5)
    polarization = lax.psum(partial_value, "energy")
    rep_start = lax.axis_index("rep") * half_rows
    col_index = lax.broadcasted_iota(jnp.int32, (half_rows, full_width), 1)
    row_index = lax.broadcasted_iota(jnp.int32, (half_rows, full_width), 0) + rep_start
    identity_rows = (col_index == row_index).astype(jnp.float32)
    identity_full = jnp.eye(full_width, dtype=jnp.float32)[None, None]
    owner_index = lax.axis_index("energy") % FREQS
    polar_own = lax.dynamic_index_in_dim(polarization, owner_index, 0, keepdims=True)
    screen_operator = identity_rows + entry_scale * coulomb[None] * polar_own
    count_own = lax.dynamic_index_in_dim(screen_steps, owner_index, 0, keepdims=True)
    screen_start = jnp.broadcast_to(identity_rows, screen_operator.shape)
    inverse = newton_rows(screen_operator, screen_start, identity_full, count_own, NW)
    inverse_full = full_rows(inverse)
    screened_own = row_product(coulomb[None], inverse_full).astype(jnp.bfloat16)
    screened = jnp.stack([broadcast(screened_own, "energy", index)[0] for index in range(FREQS)])
    self_energy = (
        jnp.sum(lowered_wide * screened.astype(jnp.float32)[:, None], axis=0) * entry_scale
    )
    neighbours = with_halo(green_blocks, (("slab", 1),), 1)
    contact = (neighbours[:, 0:1].astype(jnp.float32) + neighbours[:, 2:3].astype(jnp.float32)) * (
        0.5 * entry_scale
    )
    dyson_rows = (
        onsite_level[:, None, None, None] * identity_rows
        + hamiltonian[None]
        - self_energy
        - contact
    )
    diagonal = jnp.sum(dyson_rows * identity_rows, axis=-1)
    initial = identity_rows * (1.0 / diagonal)[..., None]
    green_next = newton_rows(dyson_rows, initial, None, green_steps, NG)
    return (green_next, screened)


def solution(mesh):
    return jax.shard_map(
        body,
        mesh=mesh,
        in_specs=(
            P("energy", "slab", "rep", None),
            P("energy"),
            P(),
            P("slab", "rep", None),
            P("slab", "rep", None),
            P("energy"),
            P("energy"),
            P(),
        ),
        out_specs=(P("energy", "slab", "rep", None), P(None, "slab", "rep", None)),
        check_vma=False,
    )
```

profile of v0, /device:TPU:0, one launch (start us, length us, event | category | flops | bytes accessed | tf_op | source)
XLA Modules:
  0.0 359.1 jit_solution(1811731379270840315)
XLA Ops:
  8.3 4.9 %collective-permute-start = (bf16[1,1,256,512]{2,3,1,0:T(8,128)(2,1)S(1)}, bf16[1,1,256,512]{2,3,1,0:T(8,128)(2,1)S(1)}, u32[]{:S(2)}, u32[]{:S(2)}) collective-permute-start(bf16[1,1,256,512]{2,3,1,0:T(8,128)(2,1)S(1)} %copy.17), channel_id=1, source_target_pairs={{0,4},{4,8},{8,12},{12,16},{16,20},{20,24},{24,28},{1,5},{5,9},{9,... | collective-permute-start | bytes 786440 | tf_op jit(solution)/shard_map/ppermute | solution.py:16
  13.2 5.5 %collective-permute-done = bf16[1,1,256,512]{2,3,1,0:T(8,128)(2,1)S(1)} collective-permute-done((bf16[1,1,256,512]{2,3,1,0:T(8,128)(2,1)S(1)}, bf16[1,1,256,512]{2,3,1,0:T(8,128)(2,1)S(1)}, u32[]{:S(2)}, u32[]{:S(2)}) %collective-permute-start) | collective-permute-done | bytes 262176 | tf_op jit(solution)/shard_map/ppermute | solution.py:16
  18.7 4.4 %collective-permute-start.1 = (bf16[1,1,256,512]{2,3,1,0:T(8,128)(2,1)S(1)}, bf16[1,1,256,512]{2,3,1,0:T(8,128)(2,1)S(1)}, u32[]{:S(2)}, u32[]{:S(2)}) collective-permute-start(bf16[1,1,256,512]{2,3,1,0:T(8,128)(2,1)S(1)} %collective-permute-done), channel_id=1, source_target_pairs={{0,4},{4,8},{8,12},{12,16},{16,20},{20,24},{24,28},{1,5},{5,9},{9,... | collective-permute-start | bytes 786440 | tf_op jit(solution)/shard_map/ppermute | solution.py:16
  23.1 4.7 %collective-permute-done.1 = bf16[1,1,256,512]{2,3,1,0:T(8,128)(2,1)S(1)} collective-permute-done((bf16[1,1,256,512]{2,3,1,0:T(8,128)(2,1)S(1)}, bf16[1,1,256,512]{2,3,1,0:T(8,128)(2,1)S(1)}, u32[]{:S(2)}, u32[]{:S(2)}) %collective-permute-start.1) | collective-permute-done | bytes 262176 | tf_op jit(solution)/shard_map/ppermute | solution.py:16
  27.8 4.4 %collective-permute-start.2 = (bf16[1,1,256,512]{2,3,1,0:T(8,128)(2,1)S(1)}, bf16[1,1,256,512]{2,3,1,0:T(8,128)(2,1)S(1)}, u32[]{:S(2)}, u32[]{:S(2)}) collective-permute-start(bf16[1,1,256,512]{2,3,1,0:T(8,128)(2,1)S(1)} %collective-permute-done.1), channel_id=1, source_target_pairs={{0,4},{4,8},{8,12},{12,16},{16,20},{20,24},{24,28},{1,5},{5,9},{9,... | collective-permute-start | bytes 786440 | tf_op jit(solution)/shard_map/ppermute | solution.py:16
  32.2 3.9 %collective-permute-done.2 = bf16[1,1,256,512]{2,3,1,0:T(8,128)(2,1)S(1)} collective-permute-done((bf16[1,1,256,512]{2,3,1,0:T(8,128)(2,1)S(1)}, bf16[1,1,256,512]{2,3,1,0:T(8,128)(2,1)S(1)}, u32[]{:S(2)}, u32[]{:S(2)}) %collective-permute-start.2) | collective-permute-done | bytes 262176 | tf_op jit(solution)/shard_map/ppermute | solution.py:16
  36.1 5.3 %collective-permute-start.3 = (bf16[1,1,256,512]{2,3,1,0:T(8,128)(2,1)S(1)}, bf16[1,1,256,512]{2,3,1,0:T(8,128)(2,1)S(1)}, u32[]{:S(2)}, u32[]{:S(2)}) collective-permute-start(bf16[1,1,256,512]{2,3,1,0:T(8,128)(2,1)S(1)} %collective-permute-done.2), channel_id=1, source_target_pairs={{0,4},{4,8},{8,12},{12,16},{16,20},{20,24},{24,28},{1,5},{5,9},{9,... | collective-permute-start | bytes 786440 | tf_op jit(solution)/shard_map/ppermute | solution.py:16
  48.7 80.2 %all-reduce.4.cloned.1.call-done = f32[2,1,256,512]{2,3,1,0:T(8,128)} async-done(((f32[2,1,256,512]{2,3,1,0:T(8,128)}), f32[2,1,256,512]{2,3,1,0:T(8,128)}) %all-reduce.4.cloned.1.call-update) | async-done | bytes 1048592 | tf_op jit(solution)/shard_map/psum | solution.py:83
  129.0 1.9 fusion.18
  132.2 19.8 %all-gather.10.cloned.1.call-done = f32[1,1,512,512]{2,3,1,0:T(8,128)} async-done(((f32[1,1,256,512]{2,3,1,0:T(8,128)}), f32[1,1,512,512]{2,3,1,0:T(8,128)}) %all-gather.10.cloned.1.call-update) | async-done | bytes 1048592 | tf_op jit(solution)/shard_map/all_gather | solution.py:46
  152.0 2.0 fusion.12
  156.2 2.1 fusion.10
  158.3 18.6 %all-gather.16.cloned.1.call-done = f32[512,512]{1,0:T(8,128)} async-done(((f32[256,512]{1,0:T(8,128)}), f32[512,512]{1,0:T(8,128)}) %all-gather.16.cloned.1.call-update) | async-done | bytes 1048592 | tf_op jit(solution)/shard_map/all_gather | solution.py:42
  176.8 3.1 fusion
  180.0 21.4 %all-gather.18.cloned.1.call-done = f32[512,512]{1,0:T(8,128)} async-done(((f32[256,512]{1,0:T(8,128)}), f32[512,512]{1,0:T(8,128)}) %all-gather.18.cloned.1.call-update) | async-done | bytes 1048592 | tf_op jit(solution)/shard_map/all_gather | solution.py:42
  201.4 3.8 %select_bitcast_fusion.1 = (bf16[1,1,256,512]{2,3,1,0:T(8,128)(2,1)}, bf16[1,1,256,512]{2,3,1,0:T(8,128)(2,1)}) fusion(pred[]{:T(512)S(6)} %eq.72, pred[]{:T(512)S(6)} %eq.76, f32[512,512]{1,0:T(8,128)} %all-gather.18.cloned.1.call-done, f32[1,256,512]{2,1,0:T(8,128)S(1)} %copy-done.4), kind=kOutput, calls=%fused_computation.41 | convolution fusion | flops 805699584 | bytes 2097154 | tf_op jit(solution)/shard_map/esij,esjk->esik/dot_general | solution.py:38
  205.3 1.6 collective-permute-start.4
  209.0 69.2 %all-reduce.6.cloned.1.call-done = (bf16[1,1,256,512]{2,3,1,0:T(8,128)(2,1)}, bf16[1,1,256,512]{2,3,1,0:T(8,128)(2,1)}) async-done(((bf16[1,1,256,512]{2,3,1,0:T(8,128)(2,1)}, bf16[1,1,256,512]{2,3,1,0:T(8,128)(2,1)}), (bf16[1,1,256,512]{2,3,1,0:T(8,128)(2,1)}, bf16[1,1,256,512]{2,3,1,0:T(8,128)(2,1)})) %all-reduce.6.cloned.1.call-update) | async-done | bytes 524304 | tf_op jit(solution)/shard_map/psum | solution.py:21
  283.4 17.7 %all-gather.12.cloned.1.call-done = f32[1,1,512,512]{2,3,1,0:T(8,128)} async-done(((f32[1,1,256,512]{2,3,1,0:T(8,128)}), f32[1,1,512,512]{2,3,1,0:T(8,128)}) %all-gather.12.cloned.1.call-update) | async-done | bytes 1048592 | tf_op jit(solution)/shard_map/all_gather | solution.py:46
  301.1 2.3 fusion.8
  303.4 21.1 %all-gather.14.cloned.1.call-done = f32[1,1,512,512]{2,3,1,0:T(8,128)} async-done(((f32[1,1,256,512]{2,3,1,0:T(8,128)}), f32[1,1,512,512]{2,3,1,0:T(8,128)}) %all-gather.14.cloned.1.call-update) | async-done | bytes 1048592 | tf_op jit(solution)/shard_map/all_gather | solution.py:42
  324.6 3.2 fusion.1
  330.4 18.8 %all-gather.20.cloned.1.call-done = f32[512,512]{1,0:T(8,128)} async-done(((f32[256,512]{1,0:T(8,128)}), f32[512,512]{1,0:T(8,128)}) %all-gather.20.cloned.1.call-update) | async-done | bytes 1048592 | tf_op jit(solution)/shard_map/all_gather | solution.py:42
  349.2 3.1 fusion.3
  (62 shorter events, 15.9 us)
Async XLA Ops:
  7.2 121.8 %all-reduce.4.cloned.1.call-start = ((), (), s32[]{:S(2)}) async-start(), calls=%async_computation | async-start | bytes 2097152 | tf_op jit(solution)/shard_map/psum | solution.py:83
  8.3 10.4 %collective-permute-start = (bf16[1,1,256,512]{2,3,1,0:T(8,128)(2,1)S(1)}, bf16[1,1,256,512]{2,3,1,0:T(8,128)(2,1)S(1)}, u32[]{:S(2)}, u32[]{:S(2)}) collective-permute-start(bf16[1,1,256,512]{2,3,1,0:T(8,128)(2,1)S(1)} %copy.17), channel_id=1, source_target_pairs={{0,4},{4,8},{8,12},{12,16},{16,20},{20,24},{24,28},{1,5},{5,9},{9,... | collective-permute-start | bytes 786440 | tf_op jit(solution)/shard_map/ppermute | solution.py:16
  18.7 9.1 %collective-permute-start.1 = (bf16[1,1,256,512]{2,3,1,0:T(8,128)(2,1)S(1)}, bf16[1,1,256,512]{2,3,1,0:T(8,128)(2,1)S(1)}, u32[]{:S(2)}, u32[]{:S(2)}) collective-permute-start(bf16[1,1,256,512]{2,3,1,0:T(8,128)(2,1)S(1)} %collective-permute-done), channel_id=1, source_target_pairs={{0,4},{4,8},{8,12},{12,16},{16,20},{20,24},{24,28},{1,5},{5,9},{9,... | collective-permute-start | bytes 786440 | tf_op jit(solution)/shard_map/ppermute | solution.py:16
  27.8 8.3 %collective-permute-start.2 = (bf16[1,1,256,512]{2,3,1,0:T(8,128)(2,1)S(1)}, bf16[1,1,256,512]{2,3,1,0:T(8,128)(2,1)S(1)}, u32[]{:S(2)}, u32[]{:S(2)}) collective-permute-start(bf16[1,1,256,512]{2,3,1,0:T(8,128)(2,1)S(1)} %collective-permute-done.1), channel_id=1, source_target_pairs={{0,4},{4,8},{8,12},{12,16},{16,20},{20,24},{24,28},{1,5},{5,9},{9,... | collective-permute-start | bytes 786440 | tf_op jit(solution)/shard_map/ppermute | solution.py:16
  36.1 11.1 %collective-permute-start.3 = (bf16[1,1,256,512]{2,3,1,0:T(8,128)(2,1)S(1)}, bf16[1,1,256,512]{2,3,1,0:T(8,128)(2,1)S(1)}, u32[]{:S(2)}, u32[]{:S(2)}) collective-permute-start(bf16[1,1,256,512]{2,3,1,0:T(8,128)(2,1)S(1)} %collective-permute-done.2), channel_id=1, source_target_pairs={{0,4},{4,8},{8,12},{12,16},{16,20},{20,24},{24,28},{1,5},{5,9},{9,... | collective-permute-start | bytes 786440 | tf_op jit(solution)/shard_map/ppermute | solution.py:16
  47.3 1.2 copy-start.4
  48.4 103.6 %all-gather.10.cloned.1.call-start = ((), (), s32[]{:S(2)}) async-start(), calls=%async_computation.1 | async-start | bytes 1572864 | tf_op jit(solution)/shard_map/all_gather | solution.py:46
  48.7 82.3 %copy-start.8 = (s32[2]{0:T(128)S(1)}, s32[2]{0:T(128)}, u32[]{:S(2)}) copy-start(s32[2]{0:T(128)} %param.15) | copy-start | bytes 28
  130.9 45.9 %all-gather.16.cloned.1.call-start = ((), (), s32[]{:S(2)}) async-start(), calls=%async_computation.4 | async-start | bytes 1572864 | tf_op jit(solution)/shard_map/all_gather | solution.py:42
  154.0 2.2 copy-start.3
  155.4 21.5 %copy-start.1 = (f32[256,512]{1,0:T(8,128)S(1)}, f32[256,512]{1,0:T(8,128)}, u32[]{:S(2)}) copy-start(f32[256,512]{1,0:T(8,128)} %fusion.4) | copy-start | bytes 1572868
  155.4 46.0 %all-gather.18.cloned.1.call-start = ((), (), s32[]{:S(2)}) async-start(), calls=%async_computation.5 | async-start | bytes 1572864 | tf_op jit(solution)/shard_map/all_gather | solution.py:42
  179.9 98.3 %all-reduce.6.cloned.1.call-start = ((), (), s32[]{:S(2)}) async-start(), calls=%async_computation.7 | async-start | bytes 1048576 | tf_op jit(solution)/shard_map/psum | solution.py:21
  180.0 28.2 %copy-start.7 = (f32[1,256,512]{2,1,0:T(8,128)S(1)}, f32[1,256,512]{2,1,0:T(8,128)}, u32[]{:S(2)}) copy-start(f32[1,256,512]{2,1,0:T(8,128)} %param.12) | copy-start | bytes 1572868
  205.2 95.9 %all-gather.12.cloned.1.call-start = ((), (), s32[]{:S(2)}) async-start(), calls=%async_computation.2 | async-start | bytes 1572864 | tf_op jit(solution)/shard_map/all_gather | solution.py:46
  205.3 74.2 %collective-permute-start.4 = (bf16[1,1,256,512]{2,3,1,0:T(8,128)(2,1)S(1)}, bf16[1,1,256,512]{2,3,1,0:T(8,128)(2,1)S(1)}, u32[]{:S(2)}, u32[]{:S(2)}) collective-permute-start(bf16[1,1,256,512]{2,3,1,0:T(8,128)(2,1)S(1)} %copy.17), channel_id=1, source_target_pairs={{0,2},{1,3},{4,6},{5,7},{8,10},{9,11},{12,14},{13,15},{16,18},{17,... | collective-permute-start | bytes 786440 | tf_op jit(solution)/shard_map/ppermute | solution.py:31
  206.9 72.6 %collective-permute-start.5 = (bf16[1,1,256,512]{2,3,1,0:T(8,128)(2,1)S(1)}, bf16[1,1,256,512]{2,3,1,0:T(8,128)(2,1)S(1)}, u32[]{:S(2)}, u32[]{:S(2)}) collective-permute-start(bf16[1,1,256,512]{2,3,1,0:T(8,128)(2,1)S(1)} %copy.17), channel_id=1, source_target_pairs={{2,0},{3,1},{6,4},{7,5},{10,8},{11,9},{14,12},{15,13},{18,16},{19,... | collective-permute-start | bytes 786440 | tf_op jit(solution)/shard_map/ppermute | solution.py:32
  280.5 44.1 %all-gather.14.cloned.1.call-start = ((), (), s32[]{:S(2)}) async-start(), calls=%async_computation.3 | async-start | bytes 1572864 | tf_op jit(solution)/shard_map/all_gather | solution.py:42
  281.4 67.8 %all-gather.20.cloned.1.call-start = ((), (), s32[]{:S(2)}) async-start(), calls=%async_computation.6 | async-start | bytes 1572864 | tf_op jit(solution)/shard_map/all_gather | solution.py:42
  324.6 3.2 copy-start.5
  324.6 3.2 copy-start.6
  327.7 1.1 copy-start
  327.7 1.6 copy-start.2
Sparse Core Ops, SparseCore 0:
  48.5 80.3 all-reduce.3
  131.1 20.8 all-gather.9
  155.5 21.2 all-gather.15
  180.1 21.2 all-gather.17
  205.3 72.8 all-reduce.5
  280.6 20.4 all-gather.11
  303.2 21.2 all-gather.13
  327.9 21.2 all-gather.19
where the time goes:
time: 360 us; the launch traced here: 359 us
  waiting for transfers between devices  281 us (78%)
  starting transfers between devices  22.3 us (6%)
  matrix products  21.9 us (6%)
  between operations  20.4 us (6%)
  other arithmetic  8.24 us (2%)
  local copies, waits for them, and re-layouts  5.22 us (1%)
    psum x1, waiting for transfers between devices, body(): polarization = lax.psum(partial_value, 'energy')  80.2 us
    all_gather x4, waiting for transfers between devices, full_rows(): return lax.all_gather(block_rows, 'rep', axis=2, tiled=True)  79.9 us
    psum x1, waiting for transfers between devices, broadcast(): return lax.psum(block, axis)  69.2 us
    all_gather x2, waiting for transfers between devices, newton_rows(): operator_full = lax.all_gather(operator, 'rep', axis=2, tiled=True)  37.5 us
    dot_general x9, matrix products, row_product(): jnp.einsum('esij,esjk->esik', first_factor, second_factor, precision=prec...  21.9 us
    ppermute x4, starting transfers between devices, from_behind(): return lax.ppermute(block, axis, route)  18.9 us
    ppermute x4, waiting for transfers between devices, from_behind(): return lax.ppermute(block, axis, route)  14.1 us
  transfers between devices with their start and end apart: 14, of which 11 were waited for; matrix products, arithmetic and copies ran while one was open for 4% of the time, Pallas kernels for 0%

commit v1 on v0

--- a/solution.py
+++ b/solution.py
@@ -8,6 +8,18 @@
 NG = 2
 NW = 2
 precise = lax.Precision.HIGHEST
+
+
+def doubled_up(value, axis, dim):
+    ways, here, step = (lax.axis_size(axis), lax.axis_index(axis), value.shape[dim])
+    line, have = (value, 1)
+    while have < ways:
+        line = jnp.concatenate(
+            [line, lax.ppermute(line, axis, [(d, (d - have) % ways) for d in range(ways)])],
+            axis=dim,
+        )
+        have = 2 * have
+    return jnp.roll(line, here * step, axis=dim)
 
 
 def from_behind(block, axis, distance):
@@ -39,7 +51,7 @@
 
 
 def full_rows(block_rows):
-    return lax.all_gather(block_rows, "rep", axis=2, tiled=True)
+    return doubled_up(block_rows, "rep", 2)
 
 
 def newton_rows(operator, initial, known_full, counts, turn_total):

time: 360 us -> 311 us (0.86)
  waiting for transfers between devices: 281 us -> 237 us
  matrix products: 21.9 us -> 14.5 us
    all_gather x4 -> x0, waiting for transfers between devices: 79.9 us -> none  [full_rows(): return lax.all_gather(block_rows, 'rep', axis=2, tiled=True)]
    ppermute x0 -> x4, waiting for transfers between devices: none -> 33.7 us  [doubled_up(): lax.ppermute(line, axis, [(d, (d - have) % ways) for d in range(ways)])]
    dot_general x9, matrix products: 21.9 us -> 14.5 us  [row_product(): jnp.einsum('esij,esjk->esik', first_factor, second_factor, precision=prec...]
    ppermute x0 -> x4, starting transfers between devices: none -> 4.09 us  [doubled_up(): lax.ppermute(line, axis, [(d, (d - have) % ways) for d in range(ways)])]
  transfers between devices with their start and end apart: 14 -> 14, of which waited for: 11 -> 10; matrix products, arithmetic and copies ran while one was open for 4% -> 4% of each run, Pallas kernels for 0% -> 0%
where the time goes in v1:
time: 311 us; the launch traced here: 310 us
  waiting for transfers between devices  237 us (76%)
  starting transfers between devices  25.9 us (8%)
  between operations  20 us (6%)
  matrix products  14.5 us (5%)
  other arithmetic  7.45 us (2%)
  local copies, waits for them, and re-layouts  4.75 us (2%)
    psum x1, waiting for transfers between devices, body(): polarization = lax.psum(partial_value, 'energy')  80.2 us
    psum x1, waiting for transfers between devices, broadcast(): return lax.psum(block, axis)  69.3 us
    all_gather x2, waiting for transfers between devices, newton_rows(): operator_full = lax.all_gather(operator, 'rep', axis=2, tiled=True)  40 us
    ppermute x4, waiting for transfers between devices, doubled_up(): lax.ppermute(line, axis, [(d, (d - have) % ways) for d in range(ways)])  33.7 us
    ppermute x4, starting transfers between devices, from_behind(): return lax.ppermute(block, axis, route)  18.9 us
    dot_general x9, matrix products, row_product(): jnp.einsum('esij,esjk->esik', first_factor, second_factor, precision=prec...  14.5 us
    ppermute x4, waiting for transfers between devices, from_behind(): return lax.ppermute(block, axis, route)  14.1 us
  transfers between devices with their start and end apart: 14, of which 10 were waited for; matrix products, arithmetic and copies ran while one was open for 4% of the time, Pallas kernels for 0%

profile of v1, /device:TPU:0, one launch (start us, length us, event | category | flops | bytes accessed | tf_op | source)
XLA Modules:
  0.0 310.0 jit_solution(5210526853564843862)
XLA Ops:
  8.3 4.9 %collective-permute-start = (bf16[1,1,256,512]{2,3,1,0:T(8,128)(2,1)S(1)}, bf16[1,1,256,512]{2,3,1,0:T(8,128)(2,1)S(1)}, u32[]{:S(2)}, u32[]{:S(2)}) collective-permute-start(bf16[1,1,256,512]{2,3,1,0:T(8,128)(2,1)S(1)} %copy.17), channel_id=1, source_target_pairs={{0,4},{4,8},{8,12},{12,16},{16,20},{20,24},{24,28},{1,5},{5,9},{9,... | collective-permute-start | bytes 786440 | tf_op jit(solution)/shard_map/ppermute | solution.py:28
  13.2 5.5 %collective-permute-done = bf16[1,1,256,512]{2,3,1,0:T(8,128)(2,1)S(1)} collective-permute-done((bf16[1,1,256,512]{2,3,1,0:T(8,128)(2,1)S(1)}, bf16[1,1,256,512]{2,3,1,0:T(8,128)(2,1)S(1)}, u32[]{:S(2)}, u32[]{:S(2)}) %collective-permute-start) | collective-permute-done | bytes 262176 | tf_op jit(solution)/shard_map/ppermute | solution.py:28
  18.7 4.4 %collective-permute-start.1 = (bf16[1,1,256,512]{2,3,1,0:T(8,128)(2,1)S(1)}, bf16[1,1,256,512]{2,3,1,0:T(8,128)(2,1)S(1)}, u32[]{:S(2)}, u32[]{:S(2)}) collective-permute-start(bf16[1,1,256,512]{2,3,1,0:T(8,128)(2,1)S(1)} %collective-permute-done), channel_id=1, source_target_pairs={{0,4},{4,8},{8,12},{12,16},{16,20},{20,24},{24,28},{1,5},{5,9},{9,... | collective-permute-start | bytes 786440 | tf_op jit(solution)/shard_map/ppermute | solution.py:28
  23.1 4.7 %collective-permute-done.1 = bf16[1,1,256,512]{2,3,1,0:T(8,128)(2,1)S(1)} collective-permute-done((bf16[1,1,256,512]{2,3,1,0:T(8,128)(2,1)S(1)}, bf16[1,1,256,512]{2,3,1,0:T(8,128)(2,1)S(1)}, u32[]{:S(2)}, u32[]{:S(2)}) %collective-permute-start.1) | collective-permute-done | bytes 262176 | tf_op jit(solution)/shard_map/ppermute | solution.py:28
  27.8 4.4 %collective-permute-start.2 = (bf16[1,1,256,512]{2,3,1,0:T(8,128)(2,1)S(1)}, bf16[1,1,256,512]{2,3,1,0:T(8,128)(2,1)S(1)}, u32[]{:S(2)}, u32[]{:S(2)}) collective-permute-start(bf16[1,1,256,512]{2,3,1,0:T(8,128)(2,1)S(1)} %collective-permute-done.1), channel_id=1, source_target_pairs={{0,4},{4,8},{8,12},{12,16},{16,20},{20,24},{24,28},{1,5},{5,9},{9,... | collective-permute-start | bytes 786440 | tf_op jit(solution)/shard_map/ppermute | solution.py:28
  32.2 3.9 %collective-permute-done.2 = bf16[1,1,256,512]{2,3,1,0:T(8,128)(2,1)S(1)} collective-permute-done((bf16[1,1,256,512]{2,3,1,0:T(8,128)(2,1)S(1)}, bf16[1,1,256,512]{2,3,1,0:T(8,128)(2,1)S(1)}, u32[]{:S(2)}, u32[]{:S(2)}) %collective-permute-start.2) | collective-permute-done | bytes 262176 | tf_op jit(solution)/shard_map/ppermute | solution.py:28
  36.1 5.3 %collective-permute-start.3 = (bf16[1,1,256,512]{2,3,1,0:T(8,128)(2,1)S(1)}, bf16[1,1,256,512]{2,3,1,0:T(8,128)(2,1)S(1)}, u32[]{:S(2)}, u32[]{:S(2)}) collective-permute-start(bf16[1,1,256,512]{2,3,1,0:T(8,128)(2,1)S(1)} %collective-permute-done.2), channel_id=1, source_target_pairs={{0,4},{4,8},{8,12},{12,16},{16,20},{20,24},{24,28},{1,5},{5,9},{9,... | collective-permute-start | bytes 786440 | tf_op jit(solution)/shard_map/ppermute | solution.py:28
  41.3 1.3 fusion.56
  48.7 80.2 %all-reduce.4.cloned.1.call-done = f32[2,1,256,512]{2,3,1,0:T(8,128)} async-done(((f32[2,1,256,512]{2,3,1,0:T(8,128)}), f32[2,1,256,512]{2,3,1,0:T(8,128)}) %all-reduce.4.cloned.1.call-update) | async-done | bytes 1048592 | tf_op jit(solution)/shard_map/psum | solution.py:95
  129.0 1.9 fusion.42
  132.2 19.8 %all-gather.3.cloned.1.call-done = f32[1,1,512,512]{2,3,1,0:T(8,128)} async-done(((f32[1,1,256,512]{2,3,1,0:T(8,128)}), f32[1,1,512,512]{2,3,1,0:T(8,128)}) %all-gather.3.cloned.1.call-update) | async-done | bytes 1048592 | tf_op jit(solution)/shard_map/all_gather | solution.py:58
  152.0 2.1 fusion.36
  156.8 11.4 %collective-permute-done.4 = f32[1,1,256,512]{3,2,1,0:T(8,128)S(1)} collective-permute-done((f32[1,1,256,512]{3,2,1,0:T(8,128)S(1)}, f32[1,1,256,512]{3,2,1,0:T(8,128)S(1)}, u32[]{:S(2)}, u32[]{:S(2)}) %collective-permute-start.4) | collective-permute-done | bytes 524320 | tf_op jit(solution)/shard_map/ppermute | solution.py:18
  168.2 1.3 fusion.1
  170.1 12.1 %collective-permute-done.5 = f32[1,1,256,512]{3,2,1,0:T(8,128)S(1)} collective-permute-done((f32[1,1,256,512]{3,2,1,0:T(8,128)S(1)}, f32[1,1,256,512]{3,2,1,0:T(8,128)S(1)}, u32[]{:S(2)}, u32[]{:S(2)}) %collective-permute-start.5) | collective-permute-done | bytes 524320 | tf_op jit(solution)/shard_map/ppermute | solution.py:18
  182.2 2.8 select_bitcast_fusion.1
  186.5 1.5 collective-permute-start.7
  188.8 69.3 %all-reduce.6.cloned.1.call-done = (bf16[1,1,256,512]{2,3,1,0:T(8,128)(2,1)}, bf16[1,1,256,512]{2,3,1,0:T(8,128)(2,1)}) async-done(((bf16[1,1,256,512]{2,3,1,0:T(8,128)(2,1)}, bf16[1,1,256,512]{2,3,1,0:T(8,128)(2,1)}), (bf16[1,1,256,512]{2,3,1,0:T(8,128)(2,1)}, bf16[1,1,256,512]{2,3,1,0:T(8,128)(2,1)})) %all-reduce.6.cloned.1.call-update) | async-done | bytes 524304 | tf_op jit(solution)/shard_map/psum | solution.py:33
  260.4 1.5 collective-permute-start.8
  263.7 20.2 %all-gather.5.cloned.1.call-done = f32[1,1,512,512]{2,3,1,0:T(8,128)} async-done(((f32[1,1,256,512]{2,3,1,0:T(8,128)}), f32[1,1,512,512]{2,3,1,0:T(8,128)}) %all-gather.5.cloned.1.call-update) | async-done | bytes 1048592 | tf_op jit(solution)/shard_map/all_gather | solution.py:58
  283.9 2.3 fusion.32
  287.6 1.5 collective-permute-start.9
  291.2 10.1 %collective-permute-done.9 = f32[1,1,256,512]{3,2,1,0:T(8,128)S(1)} collective-permute-done((f32[1,1,256,512]{3,2,1,0:T(8,128)S(1)}, f32[1,1,256,512]{3,2,1,0:T(8,128)S(1)}, u32[]{:S(2)}, u32[]{:S(2)}) %collective-permute-start.9) | collective-permute-done | bytes 524320 | tf_op jit(solution)/shard_map/ppermute | solution.py:18
  301.4 2.1 fusion.4
  (54 shorter events, 15.5 us)
Async XLA Ops:
  7.2 121.8 %all-reduce.4.cloned.1.call-start = ((), (), s32[]{:S(2)}) async-start(), calls=%async_computation | async-start | bytes 2097152 | tf_op jit(solution)/shard_map/psum | solution.py:95
  8.3 10.4 %collective-permute-start = (bf16[1,1,256,512]{2,3,1,0:T(8,128)(2,1)S(1)}, bf16[1,1,256,512]{2,3,1,0:T(8,128)(2,1)S(1)}, u32[]{:S(2)}, u32[]{:S(2)}) collective-permute-start(bf16[1,1,256,512]{2,3,1,0:T(8,128)(2,1)S(1)} %copy.17), channel_id=1, source_target_pairs={{0,4},{4,8},{8,12},{12,16},{16,20},{20,24},{24,28},{1,5},{5,9},{9,... | collective-permute-start | bytes 786440 | tf_op jit(solution)/shard_map/ppermute | solution.py:28
  18.7 9.1 %collective-permute-start.1 = (bf16[1,1,256,512]{2,3,1,0:T(8,128)(2,1)S(1)}, bf16[1,1,256,512]{2,3,1,0:T(8,128)(2,1)S(1)}, u32[]{:S(2)}, u32[]{:S(2)}) collective-permute-start(bf16[1,1,256,512]{2,3,1,0:T(8,128)(2,1)S(1)} %collective-permute-done), channel_id=1, source_target_pairs={{0,4},{4,8},{8,12},{12,16},{16,20},{20,24},{24,28},{1,5},{5,9},{9,... | collective-permute-start | bytes 786440 | tf_op jit(solution)/shard_map/ppermute | solution.py:28
  27.8 8.3 %collective-permute-start.2 = (bf16[1,1,256,512]{2,3,1,0:T(8,128)(2,1)S(1)}, bf16[1,1,256,512]{2,3,1,0:T(8,128)(2,1)S(1)}, u32[]{:S(2)}, u32[]{:S(2)}) collective-permute-start(bf16[1,1,256,512]{2,3,1,0:T(8,128)(2,1)S(1)} %collective-permute-done.1), channel_id=1, source_target_pairs={{0,4},{4,8},{8,12},{12,16},{16,20},{20,24},{24,28},{1,5},{5,9},{9,... | collective-permute-start | bytes 786440 | tf_op jit(solution)/shard_map/ppermute | solution.py:28
  36.1 11.1 %collective-permute-start.3 = (bf16[1,1,256,512]{2,3,1,0:T(8,128)(2,1)S(1)}, bf16[1,1,256,512]{2,3,1,0:T(8,128)(2,1)S(1)}, u32[]{:S(2)}, u32[]{:S(2)}) collective-permute-start(bf16[1,1,256,512]{2,3,1,0:T(8,128)(2,1)S(1)} %collective-permute-done.2), channel_id=1, source_target_pairs={{0,4},{4,8},{8,12},{12,16},{16,20},{20,24},{24,28},{1,5},{5,9},{9,... | collective-permute-start | bytes 786440 | tf_op jit(solution)/shard_map/ppermute | solution.py:28
  47.3 1.2 copy-start.4
  48.4 103.6 %all-gather.3.cloned.1.call-start = ((), (), s32[]{:S(2)}) async-start(), calls=%async_computation.1 | async-start | bytes 1572864 | tf_op jit(solution)/shard_map/all_gather | solution.py:58
  48.7 82.3 %copy-start.6 = (s32[2]{0:T(128)S(1)}, s32[2]{0:T(128)}, u32[]{:S(2)}) copy-start(s32[2]{0:T(128)} %param.17) | copy-start | bytes 28
  130.9 127.2 %all-reduce.6.cloned.1.call-start = ((), (), s32[]{:S(2)}) async-start(), calls=%async_computation.3 | async-start | bytes 1048576 | tf_op jit(solution)/shard_map/psum | solution.py:33
  152.0 3.7 %copy-start = (f32[1,1,512,512]{2,3,1,0:T(8,128)S(1)}, f32[1,1,512,512]{2,3,1,0:T(8,128)}, u32[]{:S(2)}) copy-start(f32[1,1,512,512]{2,3,1,0:T(8,128)} %all-gather.3.cloned.1.call-done) | copy-start | bytes 3145732
  154.7 13.6 %collective-permute-start.4 = (f32[1,1,256,512]{3,2,1,0:T(8,128)S(1)}, f32[1,1,256,512]{3,2,1,0:T(8,128)S(1)}, u32[]{:S(2)}, u32[]{:S(2)}) collective-permute-start(f32[1,1,256,512]{3,2,1,0:T(8,128)S(1)} %bitcast.91), channel_id=1, source_target_pairs={{0,1},{1,0},{2,3},{3,2},{4,5},{5,4},{6,7},{7,6},{8,9},{9,8},{10,11... | collective-permute-start | bytes 1572872 | tf_op jit(solution)/shard_map/ppermute | solution.py:18
  169.5 12.7 %collective-permute-start.5 = (f32[1,1,256,512]{3,2,1,0:T(8,128)S(1)}, f32[1,1,256,512]{3,2,1,0:T(8,128)S(1)}, u32[]{:S(2)}, u32[]{:S(2)}) collective-permute-start(f32[1,1,256,512]{3,2,1,0:T(8,128)S(1)} %fusion.1), channel_id=1, source_target_pairs={{0,1},{1,0},{2,3},{3,2},{4,5},{5,4},{6,7},{7,6},{8,9},{9,8},{10,11... | collective-permute-start | bytes 1572872 | tf_op jit(solution)/shard_map/ppermute | solution.py:18
  170.1 17.8 %copy-start.5 = (f32[1,256,512]{2,1,0:T(8,128)S(1)}, f32[1,256,512]{2,1,0:T(8,128)}, u32[]{:S(2)}) copy-start(f32[1,256,512]{2,1,0:T(8,128)} %param.14) | copy-start | bytes 1572868
  185.1 98.8 %all-gather.5.cloned.1.call-start = ((), (), s32[]{:S(2)}) async-start(), calls=%async_computation.2 | async-start | bytes 1572864 | tf_op jit(solution)/shard_map/all_gather | solution.py:58
  185.2 74.2 %collective-permute-start.6 = (bf16[1,1,256,512]{2,3,1,0:T(8,128)(2,1)S(1)}, bf16[1,1,256,512]{2,3,1,0:T(8,128)(2,1)S(1)}, u32[]{:S(2)}, u32[]{:S(2)}) collective-permute-start(bf16[1,1,256,512]{2,3,1,0:T(8,128)(2,1)S(1)} %copy.17), channel_id=1, source_target_pairs={{0,2},{1,3},{4,6},{5,7},{8,10},{9,11},{12,14},{13,15},{16,18},{17,... | collective-permute-start | bytes 786440 | tf_op jit(solution)/shard_map/ppermute | solution.py:43
  186.5 72.9 %collective-permute-start.7 = (bf16[1,1,256,512]{2,3,1,0:T(8,128)(2,1)S(1)}, bf16[1,1,256,512]{2,3,1,0:T(8,128)(2,1)S(1)}, u32[]{:S(2)}, u32[]{:S(2)}) collective-permute-start(bf16[1,1,256,512]{2,3,1,0:T(8,128)(2,1)S(1)} %copy.17), channel_id=1, source_target_pairs={{2,0},{3,1},{6,4},{7,5},{10,8},{11,9},{14,12},{15,13},{18,16},{19,... | collective-permute-start | bytes 786440 | tf_op jit(solution)/shard_map/ppermute | solution.py:44
  260.4 25.8 %collective-permute-start.8 = (f32[1,1,256,512]{2,3,1,0:T(8,128)S(1)}, f32[1,1,256,512]{2,3,1,0:T(8,128)S(1)}, u32[]{:S(2)}, u32[]{:S(2)}) collective-permute-start(f32[1,1,256,512]{2,3,1,0:T(8,128)S(1)} %fusion.43), channel_id=1, source_target_pairs={{0,1},{1,0},{2,3},{3,2},{4,5},{5,4},{6,7},{7,6},{8,9},{9,8},{10,11... | collective-permute-start | bytes 1572872 | tf_op jit(solution)/shard_map/ppermute | solution.py:18
  286.2 2.9 copy-start.2
  286.3 2.9 copy-start.3
  287.6 2.6 copy-start.1
  287.6 13.8 %collective-permute-start.9 = (f32[1,1,256,512]{3,2,1,0:T(8,128)S(1)}, f32[1,1,256,512]{3,2,1,0:T(8,128)S(1)}, u32[]{:S(2)}, u32[]{:S(2)}) collective-permute-start(f32[1,1,256,512]{3,2,1,0:T(8,128)S(1)} %bitcast.93), channel_id=1, source_target_pairs={{0,1},{1,0},{2,3},{3,2},{4,5},{5,4},{6,7},{7,6},{8,9},{9,8},{10,11... | collective-permute-start | bytes 1572872 | tf_op jit(solution)/shard_map/ppermute | solution.py:18
Sparse Core Ops, SparseCore 0:
  48.5 80.3 all-reduce.3
  131.1 20.8 all-gather.2
  185.2 72.8 all-reduce.5
  260.5 23.3 all-gather.4
